TPU v7x, 32 devices: a whole 2x2x4 slice. The times are simulated.
32 devices in a mesh: pair: 4 (over y, x), vtile: 8 (over z, core).
Axes of the slice: x: 2, y: 2, z: 4, core: 2. Of those that a mesh axis runs over, the one named last changes fastest.
Arguments:
- amplitudes: bfloat16 [32, 512, 512], P(('pair', 'vtile')), may hold values from -1.1953125 to 1.1953125
- factors: bfloat16 [512, 512, 2048], P('vtile', 'pair'), may hold values from -0.125 to 0.125
- pair_list: int32 [32, 2], P(('pair', 'vtile')), may hold values from 0 to 127
- window_offsets: int32 [2], replicated, may hold values from 0 to 511
- occupied_energy: float32 [128], replicated, may hold values from -3 to -0.5
- virtual_energy: float32 [512], replicated, may hold values from 0.5 to 4
Outputs:
- residual: float32 [32, 2, 512], P(('pair', 'vtile'))
- update: float32 [32, 2, 512], P(('pair', 'vtile'))
All inputs are finite; a program needn't handle non-finite values.
Results may differ from a plain program's by a relative error of at most 0.0029.
Values may be sent and summed in bfloat16 or wider, within the bound.
A program may use at most 128 MiB of HBM per device.

v0:
```python
import functools

import jax
import jax.numpy as jnp
from jax import lax
from jax.experimental import pallas as pl
from jax.experimental.pallas import tpu as pltpu
from jax.sharding import PartitionSpec as P

MESH = pl.DeviceIdType.MESH


def lookup(table, indices):
    positions = jnp.arange(table.shape[0], dtype=jnp.int32)
    return jnp.sum(jnp.where(positions[None, :] == indices[:, None], table[None, :], 0.0), axis=1)


def spread_kernel(
    pair_count, tile_count, sub,
    rows_ref, amp_ref, full_ref, mine_ref,
    core_buf, own_buf, up_buf, down_buf, up_out, down_out,
    core_sems, up_sems, down_sems, peer_sems, fwd_sems, amp_sems, local_sem,
):
    p = lax.axis_index("pair")
    t = lax.axis_index("vtile")
    core = lax.rem(t, 2)
    stage = t // 2
    stages = tile_count // 2
    window, cols, aux = rows_ref.shape
    half = aux // 2
    mate = (p, stage * 2 + (1 - core))
    above = (p, t + 2)
    below = (p, t - 2)
    relayed = pair_count == 4
    if relayed:
        across = p + 1 - 2 * lax.rem(p, 2)
        along = lax.rem(p + 2, 4)
        sources = [across, along, lax.rem(across + 2, 4)]
        peers = [(source, t) for source in sources]
    else:
        peers = [(lax.rem(p + j, pair_count), t) for j in range(1, pair_count)]
        sources = [lax.rem(p + pair_count - j, pair_count) for j in range(1, pair_count)]
    near = 2 if relayed else pair_count - 1

    barrier = pltpu.get_barrier_semaphore()
    around = [(p, lax.rem(t + 2, tile_count)), (p, lax.rem(t + tile_count - 2, tile_count))]
    for device in [mate] + peers + around:
        pl.semaphore_signal(barrier, inc=1, device_id=device, device_id_type=MESH)
    pl.semaphore_wait(barrier, pair_count + 2)

    mine_lanes = pl.ds(pl.multiple_of(core * half, half), half)
    mate_lanes = pl.ds(pl.multiple_of((1 - core) * half, half), half)
    chunks = [(k, pl.ds(s * sub, sub)) for k in range(window) for s in range(cols // sub)]
    count = len(chunks)

    def remote(src, dst, sems, index, device):
        return pltpu.make_async_remote_copy(
            src_ref=src, dst_ref=dst, send_sem=sems.at[(0,) + index], recv_sem=sems.at[(1,) + index],
            device_id=device, device_id_type=MESH,
        )

    def core_copy(h):
        k, rows = chunks[h]
        return remote(rows_ref.at[k, rows, mate_lanes], core_buf.at[k, rows], core_sems, (h,), mate)

    def up_copy(h):
        k, rows = chunks[h]
        return remote(up_out.at[k, rows], up_buf.at[k, rows], up_sems, (h,), above)

    def down_copy(h):
        k, rows = chunks[h]
        return remote(down_out.at[k, rows], down_buf.at[k, rows], down_sems, (h,), below)

    def peer_copy(h, j):
        k, rows = chunks[h]
        if j >= near:
            place = full_ref.at[k, sources[h % 2], rows, mine_lanes]
            return remote(place, place, peer_sems, (j, h), peers[1 - h % 2])
        place = full_ref.at[k, p, rows, mine_lanes]
        return remote(place, place, peer_sems, (j, h), peers[j])

    def fwd_copy(h, j):
        k, rows = chunks[h]
        source = p if j == pair_count - 1 else sources[j]
        place = full_ref.at[k, source, rows, mine_lanes]
        return remote(place, place, fwd_sems, (j, h), mate)

    def amp_copy(j):
        return remote(amp_ref.at[peers[j][0]], mine_ref.at[p], amp_sems, (j,), peers[j])

    for h in range(count):
        core_copy(h).start()
    for j in range(pair_count - 1):
        amp_copy(j).start()
    keep = pltpu.make_async_copy(amp_ref.at[p], mine_ref.at[p], local_sem)
    keep.start()

    def combine(h):
        k, rows = chunks[h]
        core_copy(h).wait_recv()
        own_buf[k, rows, :] = rows_ref[k, rows, mine_lanes] + core_buf[k, rows, :]

        @pl.when(stage == 0)
        def _():
            up_out[k, rows, :] = own_buf[k, rows, :]
            up_copy(h).start()

        @pl.when(stage == stages - 1)
        def _():
            down_out[k, rows, :] = own_buf[k, rows, :]
            down_copy(h).start()

    def go_up(h):
        k, rows = chunks[h]

        @pl.when(stage > 0)
        def _():
            up_copy(h).wait_recv()

            @pl.when(stage < stages - 1)
            def _():
                up_out[k, rows, :] = own_buf[k, rows, :] + up_buf[k, rows, :]
                up_copy(h).start()

    def go_down(h):
        k, rows = chunks[h]

        @pl.when(stage < stages - 1)
        def _():
            down_copy(h).wait_recv()

            @pl.when(stage > 0)
            def _():
                down_out[k, rows, :] = own_buf[k, rows, :] + down_buf[k, rows, :]
                down_copy(h).start()

    def finish(h):
        k, rows = chunks[h]

        @pl.when(stage == 0)
        def _():
            full_ref[k, p, rows, mine_lanes] = own_buf[k, rows, :] + down_buf[k, rows, :]

        @pl.when(stage == stages - 1)
        def _():
            full_ref[k, p, rows, mine_lanes] = own_buf[k, rows, :] + up_buf[k, rows, :]

        @pl.when(jnp.logical_and(stage > 0, stage < stages - 1))
        def _():
            full_ref[k, p, rows, mine_lanes] = (
                own_buf[k, rows, :] + up_buf[k, rows, :] + down_buf[k, rows, :]
            )

        for j in range(near):
            peer_copy(h, j).start()
        fwd_copy(h, pair_count - 1).start()

    def forward(h):
        for j in range(near):
            peer_copy(h, j).wait_recv()
            fwd_copy(h, j).start()
            if relayed and j == h % 2:
                peer_copy(h, near).start()

    def forward_far(h):
        for j in range(near, pair_count - 1):
            peer_copy(h, j).wait_recv()
            fwd_copy(h, j).start()

    lower = stage < stages // 2
    ahead, lag = 2, 3

    def early(h):
        @pl.when(lower)
        def _():
            go_up(h)

        @pl.when(jnp.logical_not(lower))
        def _():
            go_down(h)

    def late(h):
        @pl.when(lower)
        def _():
            go_down(h)

        @pl.when(jnp.logical_not(lower))
        def _():
            go_up(h)

    for h in range(count):
        combine(h)
    for step in range(-ahead, count + 2 * lag):
        if 0 <= step + ahead < count:
            early(step + ahead)
        if 0 <= step < count:
            late(step)
            finish(step)
        if 0 <= step - lag < count:
            forward(step - lag)
        if 0 <= step - 2 * lag < count:
            forward_far(step - 2 * lag)
    for h in range(count):
        core_copy(h).wait_send()

        @pl.when(stage < stages - 1)
        def _():
            up_copy(h).wait_send()

        @pl.when(stage > 0)
        def _():
            down_copy(h).wait_send()

        for j in range(pair_count - 1):
            peer_copy(h, j).wait_send()
        for j in range(pair_count):
            fwd_copy(h, j).wait()
    for j in range(pair_count - 1):
        amp_copy(j).wait()
    keep.wait()


def spread(picked, amp, pair_count, tile_count):
    window, cols, aux = picked.shape
    half = aux // 2
    sub = max(16, cols // 4)
    count = window * cols // sub
    block = pltpu.VMEM((window, cols, half), picked.dtype)
    dma = pltpu.SemaphoreType.DMA
    vmem = pl.BlockSpec(memory_space=pltpu.VMEM)
    return pl.pallas_call(
        functools.partial(spread_kernel, pair_count, tile_count, sub),
        out_shape=(
            jax.ShapeDtypeStruct((window, pair_count, cols, aux), picked.dtype),
            jax.ShapeDtypeStruct(amp.shape, amp.dtype),
        ),
        in_specs=[vmem, vmem],
        out_specs=(vmem, vmem),
        scratch_shapes=[block] * 6
        + [
            dma((2, count)), dma((2, count)), dma((2, count)),
            dma((2, pair_count - 1, count)), dma((2, pair_count, count)),
            dma((2, pair_count - 1)), dma,
        ],
        compiler_params=pltpu.CompilerParams(
            collective_id=0, has_side_effects=True, vmem_limit_bytes=32 * 1024 * 1024
        ),
    )(picked, amp)


def fold_kernel(amp_ref, int_ref, out_ref):
    @pl.when(pl.program_id(0) == 0)
    def _():
        out_ref[...] = jnp.zeros_like(out_ref)

    pairs, block, cols = amp_ref.shape
    total = out_ref[...]
    for c in range(0, block, 16):
        left = amp_ref[:, c : c + 16, :].reshape(pairs, 16 * cols)
        right = int_ref[:, c : c + 16, :].reshape(int_ref.shape[0], 16 * cols)
        total += lax.dot_general(
            left, right, (((1,), (1,)), ((), ())), preferred_element_type=jnp.float32
        )
    out_ref[...] = total


def fold(section, integrals):
    pairs, virt, cols = section.shape
    slots = integrals.shape[0]
    block = 64
    return pl.pallas_call(
        fold_kernel,
        grid=(virt // block,),
        out_shape=jax.ShapeDtypeStruct((pairs, slots), jnp.float32),
        in_specs=[
            pl.BlockSpec((pairs, block, cols), lambda i: (0, i, 0)),
            pl.BlockSpec((slots, block, cols), lambda i: (0, i, 0)),
        ],
        out_specs=pl.BlockSpec((pairs, slots), lambda i: (0, 0)),
        compiler_params=pltpu.CompilerParams(vmem_limit_bytes=56 * 1024 * 1024),
        cost_estimate=pl.CostEstimate(
            flops=2 * pairs * slots * virt * cols,
            bytes_accessed=2 * virt * cols * (pairs + slots),
            transcendentals=0,
        ),
    )(section, integrals)


def settle_kernel(pair_count, tile_count, part_ref, sum_ref, inbox, sems, local_sem):
    p = lax.axis_index("pair")
    t = lax.axis_index("vtile")
    total = pair_count * tile_count
    me = p * tile_count + t
    barrier = pltpu.get_barrier_semaphore()

    def place(offset):
        other = lax.rem(me + offset, total)
        return other // tile_count, lax.rem(other, tile_count)

    for offset in range(1, total):
        pl.semaphore_signal(barrier, inc=1, device_id=place(offset), device_id_type=MESH)
    pl.semaphore_wait(barrier, total - 1)

    def copy(offset):
        there = place(offset)
        return pltpu.make_async_remote_copy(
            src_ref=part_ref.at[there[1], there[0]], dst_ref=inbox.at[p, t],
            send_sem=sems.at[0, offset], recv_sem=sems.at[1, offset],
            device_id=there, device_id_type=MESH,
        )

    for offset in range(1, total):
        copy(offset).start()
    keep = pltpu.make_async_copy(part_ref.at[t, p], inbox.at[p, t], local_sem)
    keep.start()
    keep.wait()
    for offset in range(1, total):
        copy(offset).wait()
    added = inbox[0]
    for source in range(1, pair_count):
        added = added + inbox[source]
    sum_ref[...] = added


def settle(part):
    tile_count, pair_count, local_pairs, width = part.shape
    total = tile_count * pair_count
    vmem = pl.BlockSpec(memory_space=pltpu.VMEM)
    return pl.pallas_call(
        functools.partial(settle_kernel, pair_count, tile_count),
        out_shape=jax.ShapeDtypeStruct((tile_count, local_pairs, width), part.dtype),
        in_specs=[vmem],
        out_specs=vmem,
        scratch_shapes=[
            pltpu.VMEM((pair_count, tile_count, local_pairs, width), part.dtype),
            pltpu.SemaphoreType.DMA((2, total)),
            pltpu.SemaphoreType.DMA,
        ],
        compiler_params=pltpu.CompilerParams(collective_id=1, has_side_effects=True),
    )(part)


def local(amplitudes, factors, pair_list, window_offsets, occupied_energy, virtual_energy):
    pair_count = lax.axis_size("pair")
    tile_count = lax.axis_size("vtile")
    row_count, col_count, aux_count = factors.shape
    window_count = window_offsets.shape[0]
    local_pairs, virt_count = (amplitudes.shape[0], amplitudes.shape[1])
    local_rows = window_offsets % row_count
    owned = (window_offsets // row_count) == lax.axis_index("vtile")
    picked = jnp.stack(
        [
            lax.dynamic_index_in_dim(factors, local_rows[slot_index], 0, keepdims=False)
            for slot_index in range(window_count)
        ]
    )
    picked = jnp.where(owned[:, None, None], picked, jnp.zeros_like(picked))
    amp = amplitudes.reshape(local_pairs, virt_count, pair_count, col_count).transpose(2, 0, 1, 3)
    arows, mine = spread(picked, amp, pair_count, tile_count)
    arows = arows.reshape(window_count, virt_count, aux_count)
    mine = mine.reshape(pair_count * local_pairs, virt_count, col_count)
    section = lax.all_gather(mine, "vtile", axis=0, tiled=True)
    integrals = jnp.einsum(
        "acq,bdq->abcd", arows, factors, preferred_element_type=jnp.float32
    ).astype(jnp.bfloat16)
    folded = fold(
        section, integrals.reshape(window_count * row_count, virt_count, col_count)
    )
    summed = settle(
        folded.reshape(tile_count, pair_count, local_pairs, window_count * row_count)
    )
    residual = (
        summed.reshape(tile_count, local_pairs, window_count, row_count)
        .transpose(1, 2, 0, 3)
        .reshape(local_pairs, window_count, virt_count)
    )
    occupied_sum = lookup(occupied_energy, pair_list[:, 0]) + lookup(
        occupied_energy, pair_list[:, 1]
    )
    window_energy = lookup(virtual_energy, window_offsets)
    denominator = (
        window_energy[None, :, None] + virtual_energy[None, None, :] - occupied_sum[:, None, None]
    )
    update = residual / denominator
    return (residual, update)


def solution(mesh):
    return jax.shard_map(
        local,
        mesh=mesh,
        in_specs=(
            P(("pair", "vtile"), None, None),
            P("vtile", "pair", None),
            P(("pair", "vtile"), None),
            P(),
            P(),
            P(),
        ),
        out_specs=(P(("pair", "vtile"), None, None), P(("pair", "vtile"), None, None)),
        check_vma=False,
    )
```

profile of v0, /device:TPU:0, one launch (start us, length us, event | category | flops | bytes accessed | tf_op | source)
XLA Modules:
  0.0 138.2 jit_solution(9495174075067089906)
XLA Ops:
  7.2 0.0 all-gather.3.cloned.1.call-start
  7.2 0.7 and_select_fusion
  7.9 0.6 fusion.10
  11.1 0.7 fusion.8
  11.7 1.3 copy.17
  13.0 0.3 copy.18
  14.6 1.3 constant_dynamic-slice_fusion.1
  15.8 0.2 maximum_select_fusion.rows_ref
  16.0 40.1 %shard_map.77 = (bf16[2,4,128,2048]{3,2,1,0:T(8,128)(2,1)S(1)}, bf16[4,1,512,128]{3,2,1,0:T(8,128)(2,1)}) custom-call(bf16[2,128,2048]{2,1,0:T(8,128)(2,1)S(1)} %maximum_select_fusion.rows_ref, bf16[4,1,512,128]{3,2,1,0:T(8,128)(2,1)S(1)} %bitcast.25), custom_call_target="tpu_custom_call" | custom-call | tf_op jit(solution)/shard_map/pallas_call | solution.py:231
  56.1 0.0 copy-start
  56.1 2.0 %copy-done = bf16[2,4,128,2048]{3,2,1,0:T(8,128)(2,1)} copy-done((bf16[2,4,128,2048]{3,2,1,0:T(8,128)(2,1)}, bf16[2,4,128,2048]{3,2,1,0:T(8,128)(2,1)S(1)}, u32[]{:S(2)}) %copy-start) | copy-done | bytes 4194328
  58.1 0.0 all-gather.3.cloned.1.call-update
  58.1 1.3 fusion.9
  59.4 2.6 %fusion.7 = (f32[]{:T(128)}, f32[]{:T(128)}) fusion(f32[128]{0:T(128)} %param.10, s32[]{:T(128)} %bitcast.14, s32[]{:T(128)} %bitcast.13), kind=kLoop, calls=%fused_computation.15 | loop fusion | flops 766 | bytes 528 | tf_op jit(solution)/shard_map/reduce_sum | solution.py:15
  63.3 0.9 fusion.5
  64.2 41.5 %fusion.2 = bf16[2,512,64,128]{3,1,2,0:T(8,128)(2,1)} fusion(bf16[2,512,2048,1]{2,1,3,0:T(8,128)(2,1)} %bitcast.26, bf16[64,128,2048]{2,1,0:T(8,128)(2,1)} %param.7), kind=kOutput, calls=%fused_computation.2 | convolution fusion | flops 34368126976 | bytes 54525952 | tf_op jit(solution)/shard_map/acq,bdq->abcd/dot_general | solution.py:363
  105.7 0.0 copy-start.2
  105.7 0.0 all-gather.3.cloned.1.call-done
  105.7 13.6 %shard_map.78 = f32[32,128]{1,0:T(8,128)} custom-call(bf16[32,512,128]{2,1,0:T(8,128)(2,1)} %bitcast.28, bf16[128,512,128]{2,1,0:T(8,128)(2,1)} %bitcast.27), custom_call_target="tpu_custom_call" | custom-call | flops 536870912 | bytes 20971520 | tf_op jit(solution)/shard_map/pallas_call | solution.py:271
  119.3 9.4 %shard_map.79 = f32[8,1,128]{2,1,0:T(1,128)} custom-call(f32[8,4,1,128]{3,2,1,0:T(1,128)} %bitcast.30), custom_call_target="tpu_custom_call" | custom-call | tf_op jit(solution)/shard_map/pallas_call | solution.py:329
  128.7 0.5 broadcast.92
  129.2 1.3 reduce.7
  130.5 0.1 reshape.114
  130.6 0.1 reshape.115
  130.7 0.0 copy-done.2
  130.7 0.0 copy-start.1
  130.7 0.7 subtract_divide_fusion
  131.3 0.0 copy-done.1
  (1 shorter events, 0.0 us)
Async XLA Ops:
  7.2 98.5 %all-gather.3.cloned.1.call-start = ((), (), s32[]{:S(2)}) async-start(), calls=%async_computation | async-start | bytes 4718592 | tf_op jit(solution)/shard_map/all_gather | solution.py:362
  56.1 2.0 %copy-start = (bf16[2,4,128,2048]{3,2,1,0:T(8,128)(2,1)}, bf16[2,4,128,2048]{3,2,1,0:T(8,128)(2,1)S(1)}, u32[]{:S(2)}) copy-start(bf16[2,4,128,2048]{3,2,1,0:T(8,128)(2,1)S(1)} %get-tuple-element.5) | copy-start | bytes 12582916
  105.7 25.0 %copy-start.2 = (f32[512]{0:T(512)S(1)}, f32[512]{0:T(512)}, u32[]{:S(2)}) copy-start(f32[512]{0:T(512)} %param.11) | copy-start | bytes 6148
  130.7 0.7 copy-start.1
Sparse Core Ops, SparseCore 0:
  58.2 45.8 all-gather.2
where the time goes:
time: 139 us; the launch traced here: 138 us
  Pallas kernels  63 us (45%)
  matrix products  41.5 us (30%)
  between operations  19.2 us (14%)
  local copies, waits for them, and re-layouts  7.34 us (5%)
  other arithmetic  7.04 us (5%)
    dot_general x1, matrix products, local(): jnp.einsum('acq,bdq->abcd', arows, factors, preferred_element_type=jnp.fl...  41.5 us
    pallas_call x1, Pallas kernels, spread(): pl.pallas_call(functools.partial(spread_kernel, pair_count, tile_count, s...  40.1 us
    pallas_call x1, Pallas kernels, fold(): pl.pallas_call(fold_kernel, grid=(virt // block,), out_shape=jax.ShapeDty...  13.6 us
    pallas_call x1, Pallas kernels, settle(): pl.pallas_call(functools.partial(settle_kernel, pair_count, tile_count),...  9.36 us
    reduce_sum x2, other arithmetic, lookup(): jnp.sum(jnp.where(positions[None, :] == indices[:, None], table[None, :],...  3.52 us
    unnamed x7, local copies, waits for them, and re-layouts  3.22 us
  transfers between devices with their start and end apart: 1, of which 0 were waited for; matrix products, arithmetic and copies ran while one was open for 34% of the time, Pallas kernels for 0%

commit v1 on v0

v1 whole, which is shorter than its diff:
```python
import functools

import jax
import jax.numpy as jnp
from jax import lax
from jax.experimental import pallas as pl
from jax.experimental.pallas import tpu as pltpu
from jax.sharding import PartitionSpec as P

MESH = pl.DeviceIdType.MESH
VMEM = pl.BlockSpec(memory_space=pltpu.VMEM)
SMEM = pl.BlockSpec(memory_space=pltpu.SMEM)
F32 = jnp.float32
GROUP = 16


def prepare_kernel(
    offsets_ref, pairs_ref, occupied_ref, energy_ref, virtual_ref, factors_ref, amp_ref,
    rows_ref, turned_ref, den_ref, sems,
):
    t = lax.axis_index("vtile")
    row_count = factors_ref.shape[0]
    window = rows_ref.shape[0]

    def local_row(k):
        return offsets_ref[k] - t * row_count

    def pick(k):
        row = jnp.clip(local_row(k), 0, row_count - 1)
        return pltpu.make_async_copy(factors_ref.at[row], rows_ref.at[k], sems.at[k])

    for k in range(window):
        pick(k).start()
    for pair in range(amp_ref.shape[0]):
        turned_ref[pair] = amp_ref[pair].T
        occupied = occupied_ref[pairs_ref[pair, 0]] + occupied_ref[pairs_ref[pair, 1]]
        for k in range(window):
            den_ref[pair, k : k + 1, :] = (energy_ref[offsets_ref[k]] + virtual_ref[...]) - occupied
    for k in range(window):
        pick(k).wait()
        row = local_row(k)

        @pl.when(jnp.logical_or(row < 0, row >= row_count))
        def _():
            rows_ref[k] = jnp.zeros(rows_ref.shape[1:], rows_ref.dtype)


def prepare(amplitudes, factors, pair_list, window_offsets, occupied_energy, virtual_energy):
    local_pairs, virt, _ = amplitudes.shape
    window = window_offsets.shape[0]
    return pl.pallas_call(
        prepare_kernel,
        out_shape=(
            jax.ShapeDtypeStruct((window,) + factors.shape[1:], factors.dtype),
            jax.ShapeDtypeStruct(amplitudes.shape, amplitudes.dtype),
            jax.ShapeDtypeStruct((local_pairs, window, virt), F32),
        ),
        in_specs=[SMEM, SMEM, SMEM, SMEM, VMEM, pl.BlockSpec(memory_space=pl.ANY), VMEM],
        out_specs=(VMEM, VMEM, VMEM),
        scratch_shapes=[pltpu.SemaphoreType.DMA((window,))],
    )(
        window_offsets, pair_list, occupied_energy, virtual_energy,
        virtual_energy.reshape(1, virt), factors, amplitudes,
    )


def ladder_kernel(
    pair_count, tile_count, sub, width,
    rows_ref, turned_ref, den_ref, factors_ref,
    res_ref, upd_ref, land_ref,
    full, core_buf, own_buf, up_buf, down_buf, up_out, down_out,
    taus, sorted_taus, stage_buf, table, swap, half_made, acc, part, inbox,
    core_sems, up_sems, down_sems, peer_sems,
    plane_sems, direct_sems, arrive_sems, relay_sems, mate_sems,
    slab_sems, stage_sems, settle_sems, local_sems,
):
    p = lax.axis_index("pair")
    t = lax.axis_index("vtile")
    core = lax.rem(t, 2)
    stage = t // 2
    stages = tile_count // 2
    total = pair_count * tile_count
    me = p * tile_count + t
    window, cols, aux = rows_ref.shape
    half = aux // 2
    own_b, own_d, _ = factors_ref.shape
    both_b = 2 * own_b
    local_pairs = turned_ref.shape[0]
    block = pair_count * local_pairs
    pairs = tile_count * block
    steps = own_d // GROUP
    spread = swap.shape[0]
    mate = (p, stage * 2 + (1 - core))
    above = (p, t + 2)
    below = (p, t - 2)
    relayed = pair_count == 4
    if relayed:
        across = p + 1 - 2 * lax.rem(p, 2)
        along = lax.rem(p + 2, 4)
        sources = [across, along, lax.rem(across + 2, 4)]
        peers = [(source, t) for source in sources]
    else:
        peers = [(lax.rem(p + j, pair_count), t) for j in range(1, pair_count)]
        sources = [lax.rem(p + pair_count - j, pair_count) for j in range(1, pair_count)]
    near = 2 if relayed else pair_count - 1

    def place(offset):
        other = lax.rem(me + offset, total)
        return other // tile_count, lax.rem(other, tile_count)

    barrier = pltpu.get_barrier_semaphore()
    for offset in range(1, total):
        pl.semaphore_signal(barrier, inc=1, device_id=place(offset), device_id_type=MESH)
    pl.semaphore_wait(barrier, total - 1)

    mine_lanes = pl.ds(pl.multiple_of(core * half, half), half)
    mate_lanes = pl.ds(pl.multiple_of((1 - core) * half, half), half)
    chunks = [(k, pl.ds(s * sub, sub)) for k in range(window) for s in range(cols // sub)]
    count = len(chunks)

    def remote(src, dst, sems, index, device):
        return pltpu.make_async_remote_copy(
            src_ref=src, dst_ref=dst, send_sem=sems.at[(0,) + index], recv_sem=sems.at[(1,) + index],
            device_id=device, device_id_type=MESH,
        )

    def group(i):
        return pl.ds(pl.multiple_of(i * GROUP, GROUP), GROUP)

    def core_copy(h):
        k, rows = chunks[h]
        return remote(rows_ref.at[k, rows, mate_lanes], core_buf.at[k, rows], core_sems, (h,), mate)

    def up_copy(h):
        k, rows = chunks[h]
        return remote(up_out.at[k, rows], up_buf.at[k, rows], up_sems, (h,), above)

    def down_copy(h):
        k, rows = chunks[h]
        return remote(down_out.at[k, rows], down_buf.at[k, rows], down_sems, (h,), below)

    def peer_copy(h, j):
        k, rows = chunks[h]
        if j >= near:
            spot = full.at[k, sources[h % 2], rows]
            return remote(spot, spot, peer_sems, (j, h), peers[1 - h % 2])
        spot = full.at[k, p, rows]
        return remote(spot, spot, peer_sems, (j, h), peers[j])

    def plane_copy(j):
        rows = pl.ds(pl.multiple_of(peers[j][0] * own_d, own_d), own_d)
        spot = taus.at[pl.ds((t * pair_count + p) * local_pairs, local_pairs)]
        return remote(turned_ref.at[:, rows], spot, plane_sems, (j,), peers[j])

    def plane_keep():
        rows = pl.ds(pl.multiple_of(p * own_d, own_d), own_d)
        spot = taus.at[pl.ds((t * pair_count + p) * local_pairs, local_pairs)]
        return pltpu.make_async_copy(turned_ref.at[:, rows], spot, local_sems.at[0])

    def tau_spot(tile, i):
        return taus.at[pl.ds(tile * block, block), group(i)]

    shifts = [shift for shift in (-2, -1, 1, 2) if abs(shift) < stages]

    def in_range(shift):
        return jnp.logical_and(stage + shift >= 0, stage + shift < stages)

    def direct_copy(d, i):
        return pltpu.make_async_remote_copy(
            src_ref=tau_spot(t, i), dst_ref=tau_spot(t, i),
            send_sem=direct_sems.at[d, i], recv_sem=arrive_sems.at[stage, i],
            device_id=(p, t + 2 * shifts[d]), device_id_type=MESH,
        )

    def relay_copy(source, i, shift):
        spot = tau_spot(2 * source + core, i)
        return pltpu.make_async_remote_copy(
            src_ref=spot, dst_ref=spot,
            send_sem=relay_sems.at[source, i], recv_sem=arrive_sems.at[source, i],
            device_id=(p, t + 2 * shift), device_id_type=MESH,
        )

    def mate_copy(source, i):
        spot = tau_spot(2 * source + core, i)
        return remote(spot, spot, mate_sems, (source, i), mate)

    def goes_up(source):
        return jnp.logical_and(stage >= source + 2, stage + 1 < stages)

    def goes_down(source):
        return jnp.logical_and(stage <= source - 2, stage >= 1)

    def send_own(i):
        for d, shift in enumerate(shifts):
            @pl.when(in_range(shift))
            def _():
                direct_copy(d, i).start()

    def relay(i):
        for source in range(stages):
            @pl.when(goes_up(source))
            def _():
                relay_copy(source, i, 1).wait_recv()
                relay_copy(source, i, 1).start()

            @pl.when(goes_down(source))
            def _():
                relay_copy(source, i, -1).wait_recv()
                relay_copy(source, i, -1).start()

    def collect(i):
        for source in range(stages):
            passed = jnp.logical_or(goes_up(source), goes_down(source))

            @pl.when(jnp.logical_not(jnp.logical_or(passed, stage == source)))
            def _():
                relay_copy(source, i, 1).wait_recv()

            mate_copy(source, i).start()

    def slab_copy(i):
        return remote(
            factors_ref.at[:, group(i), mate_lanes], land_ref.at[:, group(i)], slab_sems, (i,), mate
        )

    slots = stage_buf.shape[0]

    def own_load(i, slot):
        return pltpu.make_async_copy(
            factors_ref.at[:, group(i), mine_lanes], stage_buf.at[slot], stage_sems.at[slot]
        )

    def mate_load(i, slot):
        return pltpu.make_async_copy(land_ref.at[:, group(i)], stage_buf.at[slot], stage_sems.at[slot])

    def sort_slab(i, slot, side):
        def one(b, carry):
            rows = stage_buf[slot, group(b)].reshape(GROUP * GROUP, half)
            made = jnp.dot(swap[...], rows, preferred_element_type=F32).astype(table.dtype)
            spot = pl.ds(pl.multiple_of(side * own_b + b * GROUP, GROUP), GROUP)
            table[group(i), spot, :] = made.reshape(GROUP, GROUP, half)
            return carry

        lax.fori_loop(0, own_b // GROUP, one, 0)

    def load_slab(n):
        if n < steps:
            own_load(n, n % slots).start()
        else:
            slab_copy(n - steps).wait_recv()
            mate_load(n - steps, n % slots).start()

    def finish_slab(n):
        if n < steps:
            own_load(n, n % slots).wait()
            sort_slab(n, n % slots, core)
        else:
            mate_load(n - steps, n % slots).wait()
            sort_slab(n - steps, n % slots, 1 - core)

    first = steps + steps // 2
    early_slabs = steps - steps // 2 + 1

    for h in range(count):
        core_copy(h).start()
    for j in range(pair_count - 1):
        plane_copy(j).start()
    plane_keep().start()
    for i in range(min(early_slabs, steps)):
        slab_copy(i).start()
    for n in range(slots - 1):
        load_slab(n)
    lanes = lax.broadcasted_iota(jnp.int32, (spread, spread), 1)
    lines = lax.broadcasted_iota(jnp.int32, (spread, spread), 0)
    swap[...] = jnp.where(
        jnp.logical_and(lines // GROUP == lanes % GROUP, lines % GROUP == lanes // GROUP), 1.0, 0.0
    ).astype(swap.dtype)
    acc[...] = jnp.zeros_like(acc)

    def combine(h):
        k, rows = chunks[h]
        core_copy(h).wait_recv()
        own_buf[k, rows, :] = rows_ref[k, rows, mine_lanes] + core_buf[k, rows, :]

        @pl.when(stage == 0)
        def _():
            up_out[k, rows, :] = own_buf[k, rows, :]
            up_copy(h).start()

        @pl.when(stage == stages - 1)
        def _():
            down_out[k, rows, :] = own_buf[k, rows, :]
            down_copy(h).start()

    def go_up(h):
        k, rows = chunks[h]

        @pl.when(stage > 0)
        def _():
            up_copy(h).wait_recv()

            @pl.when(stage < stages - 1)
            def _():
                up_out[k, rows, :] = own_buf[k, rows, :] + up_buf[k, rows, :]
                up_copy(h).start()

    def go_down(h):
        k, rows = chunks[h]

        @pl.when(stage < stages - 1)
        def _():
            down_copy(h).wait_recv()

            @pl.when(stage > 0)
            def _():
                down_out[k, rows, :] = own_buf[k, rows, :] + down_buf[k, rows, :]
                down_copy(h).start()

    def finish(h):
        k, rows = chunks[h]

        @pl.when(stage == 0)
        def _():
            full[k, p, rows, :] = own_buf[k, rows, :] + down_buf[k, rows, :]

        @pl.when(stage == stages - 1)
        def _():
            full[k, p, rows, :] = own_buf[k, rows, :] + up_buf[k, rows, :]

        @pl.when(jnp.logical_and(stage > 0, stage < stages - 1))
        def _():
            full[k, p, rows, :] = own_buf[k, rows, :] + up_buf[k, rows, :] + down_buf[k, rows, :]

        for j in range(near):
            peer_copy(h, j).start()

    def forward(h):
        for j in range(near):
            peer_copy(h, j).wait_recv()
            if relayed and j == h % 2:
                peer_copy(h, near).start()

    def forward_far(h):
        for j in range(near, pair_count - 1):
            peer_copy(h, j).wait_recv()

    lower = stage < stages // 2
    ahead, lag = 2, 2

    def early(h):
        @pl.when(lower)
        def _():
            go_up(h)

        @pl.when(jnp.logical_not(lower))
        def _():
            go_down(h)

    def late(h):
        @pl.when(lower)
        def _():
            go_down(h)

        @pl.when(jnp.logical_not(lower))
        def _():
            go_up(h)

    for h in range(count):
        combine(h)
    sorted_count = 0
    for step in range(-ahead, count + 2 * lag):
        if 0 <= step + ahead < count:
            early(step + ahead)
        if 0 <= step < count:
            late(step)
            finish(step)
        if 0 <= step - lag < count:
            forward(step - lag)
        if 0 <= step - 2 * lag < count:
            forward_far(step - 2 * lag)
        if step == 1:
            for j in range(pair_count - 1):
                plane_copy(j).wait_recv()
            plane_keep().wait()
            send_own(0)
        if step == 4:
            send_own(1)
        if step == count - 1:
            send_own(2)
            relay(0)
        if sorted_count < first:
            if sorted_count + slots - 1 < first:
                load_slab(sorted_count + slots - 1)
            finish_slab(sorted_count)
            sorted_count += 1
    while sorted_count < first:
        if sorted_count + slots - 1 < first:
            load_slab(sorted_count + slots - 1)
        finish_slab(sorted_count)
        sorted_count += 1

    blocks = pairs // GROUP
    many = width // both_b
    tile = half_made.shape[-1]

    def main(i, carry):
        @pl.when(i + 3 < steps)
        def _():
            send_own(i + 3)

        @pl.when(i + 1 < steps)
        def _():
            relay(i + 1)

        collect(i)

        @pl.when(i + early_slabs < steps)
        def _():
            slab_copy(i + early_slabs).start()

        late_slab = i + first - steps

        @pl.when(late_slab < steps)
        def _():
            slab_copy(late_slab).wait_recv()
            mate_load(late_slab, 0).start()

        for source in range(stages):
            mate_copy(source, i).wait_recv()
        for s in range(blocks):
            rows = taus[s * GROUP : (s + 1) * GROUP, group(i), :].reshape(spread, -1)
            sorted_taus[s] = jnp.dot(swap[...], rows, preferred_element_type=F32).astype(taus.dtype)
        left = sorted_taus[...].reshape(blocks * spread, -1)

        def part_of(j, inner):
            qs = pl.ds(pl.multiple_of(j * tile, tile), tile)
            for k in range(window):
                right = full[k, :, :, qs].reshape(pair_count * cols, tile)
                made = jnp.dot(left, right, preferred_element_type=F32).astype(half_made.dtype)
                made = made.reshape(blocks, GROUP // many, many * GROUP, tile)
                for u in range(GROUP // many):
                    half_made[u, k] = made[:, u]
            added = acc[...]
            for u in range(GROUP // many):
                right = table[pl.ds(i * GROUP + u * many, many), :, qs].reshape(width, tile)
                added += lax.dot_general(
                    half_made[u].reshape(-1, tile), right, (((1,), (1,)), ((), ())),
                    preferred_element_type=F32,
                )
            acc[...] = added
            return inner

        lax.fori_loop(0, half // tile, part_of, 0)

        @pl.when(late_slab < steps)
        def _():
            mate_load(late_slab, 0).wait()
            sort_slab(late_slab, 0, 1 - core)

        return carry

    lax.fori_loop(0, steps, main, 0)

    for k in range(window):
        for s in range(blocks):
            base = (k * blocks + s) * many * GROUP
            value = acc[base : base + GROUP, 0:both_b]
            for u in range(1, many):
                value += acc[base + u * GROUP : base + (u + 1) * GROUP, u * both_b : (u + 1) * both_b]
            part[s * GROUP : (s + 1) * GROUP, k, :] = value

    def settle_copy(offset):
        there = place(offset)
        spot = pl.ds((there[1] * pair_count + there[0]) * local_pairs, local_pairs)
        return pltpu.make_async_remote_copy(
            src_ref=part.at[spot], dst_ref=inbox.at[t, p],
            send_sem=settle_sems.at[0, offset], recv_sem=settle_sems.at[1, offset],
            device_id=there, device_id_type=MESH,
        )

    for offset in range(1, total):
        settle_copy(offset).start()
    spot = pl.ds((t * pair_count + p) * local_pairs, local_pairs)
    settle_keep = pltpu.make_async_copy(part.at[spot], inbox.at[t, p], local_sems.at[1])
    settle_keep.start()

    for h in range(count):
        core_copy(h).wait_send()

        @pl.when(stage < stages - 1)
        def _():
            up_copy(h).wait_send()

        @pl.when(stage > 0)
        def _():
            down_copy(h).wait_send()

        for j in range(pair_count - 1):
            peer_copy(h, j).wait_send()
    for j in range(pair_count - 1):
        plane_copy(j).wait_send()

    def drain(i, carry):
        slab_copy(i).wait_send()
        for d, shift in enumerate(shifts):
            @pl.when(in_range(shift))
            def _():
                direct_copy(d, i).wait_send()

        for source in range(stages):
            mate_copy(source, i).wait_send()

            @pl.when(jnp.logical_or(goes_up(source), goes_down(source)))
            def _():
                relay_copy(source, i, 1).wait_send()

        return carry

    lax.fori_loop(0, steps, drain, 0)
    settle_keep.wait()
    for offset in range(1, total):
        settle_copy(offset).wait()
    for z in range(stages):
        value = inbox[2 * z, 0]
        for tile_index in (2 * z, 2 * z + 1):
            for source in range(pair_count):
                if tile_index > 2 * z or source:
                    value += inbox[tile_index, source]
        res_ref[:, :, z * both_b : (z + 1) * both_b] = value
    upd_ref[...] = res_ref[...] / den_ref[...]


def ladder(rows, turned, den, factors, pair_count, tile_count):
    window, cols, aux = rows.shape
    half = aux // 2
    own_b, own_d, _ = factors.shape
    local_pairs, virt, _ = turned.shape
    pairs = pair_count * tile_count * local_pairs
    both_b = 2 * own_b
    width = max(256, both_b)
    many = width // both_b
    sub = max(16, cols // 4)
    count = window * cols // sub
    steps = own_d // GROUP
    stages = tile_count // 2
    spread = GROUP * GROUP
    blocks = pairs // GROUP
    tile = min(512, half)
    total = pair_count * tile_count
    kind = rows.dtype
    dma = pltpu.SemaphoreType.DMA
    hbm = pl.BlockSpec(memory_space=pl.ANY)
    piece = pltpu.VMEM((window, cols, half), kind)
    shape = jax.ShapeDtypeStruct((local_pairs, window, virt), F32)
    slots = 3
    return pl.pallas_call(
        functools.partial(ladder_kernel, pair_count, tile_count, sub, width),
        out_shape=(shape, shape, jax.ShapeDtypeStruct((own_b, own_d, half), kind)),
        in_specs=[VMEM, VMEM, VMEM, hbm],
        out_specs=(VMEM, VMEM, pl.BlockSpec(memory_space=pltpu.HBM)),
        scratch_shapes=[pltpu.VMEM((window, pair_count, cols, half), kind)]
        + [piece] * 6
        + [
            pltpu.VMEM((pairs, own_d, virt), kind),
            pltpu.VMEM((blocks, spread, virt), kind),
            pltpu.VMEM((slots, own_b, GROUP, half), kind),
            pltpu.VMEM((own_d, both_b, half), kind),
            pltpu.VMEM((spread, spread), kind),
            pltpu.VMEM((GROUP // many, window, blocks, many * GROUP, tile), kind),
            pltpu.VMEM((window * blocks * many * GROUP, width), F32),
            pltpu.VMEM((pairs, window, both_b), F32),
            pltpu.VMEM((tile_count, pair_count, local_pairs, window, both_b), F32),
            dma((2, count)), dma((2, count)), dma((2, count)), dma((2, pair_count - 1, count)),
            dma((2, pair_count - 1)), dma((4, steps)), dma((stages, steps)), dma((stages, steps)),
            dma((2, stages, steps)), dma((2, steps)), dma((slots,)), dma((2, total)), dma((2,)),
        ],
        compiler_params=pltpu.CompilerParams(
            collective_id=0, has_side_effects=True, vmem_limit_bytes=63 * 1024 * 1024
        ),
    )(rows, turned, den, factors)


def local(amplitudes, factors, pair_list, window_offsets, occupied_energy, virtual_energy):
    pair_count = lax.axis_size("pair")
    tile_count = lax.axis_size("vtile")
    rows, turned, den = prepare(
        amplitudes, factors, pair_list, window_offsets, occupied_energy, virtual_energy
    )
    residual, update, _ = ladder(rows, turned, den, factors, pair_count, tile_count)
    return residual, update


def solution(mesh):
    return jax.shard_map(
        local,
        mesh=mesh,
        in_specs=(
            P(("pair", "vtile"), None, None),
            P("vtile", "pair", None),
            P(("pair", "vtile"), None),
            P(),
            P(),
            P(),
        ),
        out_specs=(P(("pair", "vtile"), None, None), P(("pair", "vtile"), None, None)),
        check_vma=False,
    )
```

time: 139 us -> 115 us (0.83)
  Pallas kernels: 63 us -> 112 us
  matrix products: 41.5 us -> 0 us
  between operations: 19.2 us -> 0.65 us
  other arithmetic: 7.04 us -> 0 us
  local copies, waits for them, and re-layouts: 7.34 us -> 2.53 us
    pallas_call x3 -> x2, Pallas kernels: 63 us -> 112 us  [the longest x1 108 us: ladder(): pl.pallas_call(functools.partial(ladder_kernel, pair_count, tile_count, s...]
    dot_general x1 -> x0, matrix products: 41.5 us -> none  [local(): jnp.einsum('acq,bdq->abcd', arows, factors, preferred_element_type=jnp.fl...]
    reduce_sum x2 -> x0, other arithmetic: 3.52 us -> none  [lookup(): jnp.sum(jnp.where(positions[None, :] == indices[:, None], table[None, :],...]
    slice x2 -> x0, local copies, waits for them, and re-layouts: 1.9 us -> none  [the longest x1 1.31 us: local(): pair_list[:, 0]]
    unnamed x7 -> x2, local copies, waits for them, and re-layouts: 3.22 us -> 2.53 us
  transfers between devices with their start and end apart: 1 -> 0, of which waited for: 0 -> 0; matrix products, arithmetic and copies ran while one was open for 34% -> 0% of each run, Pallas kernels for 0% -> 0%
where the time goes in v1:
time: 115 us
  Pallas kernels  112 us (97%)
  local copies, waits for them, and re-layouts  2.53 us (2%)
    pallas_call x1, Pallas kernels, ladder(): pl.pallas_call(functools.partial(ladder_kernel, pair_count, tile_count, s...  108 us
    pallas_call x1, Pallas kernels, prepare(): pl.pallas_call(prepare_kernel, out_shape=(jax.ShapeDtypeStruct((window,)...  3.52 us
    unnamed x2, local copies, waits for them, and re-layouts  2.53 us

profile of v1, /device:TPU:0, one launch (start us, length us, event | category | flops | bytes accessed | tf_op | source)
XLA Modules:
  0.0 114.7 jit_solution(2574141229381205888)
XLA Ops:
  0.6 3.5 %shard_map.77 = (bf16[2,128,2048]{2,1,0:T(8,128)(2,1)}, bf16[1,512,512]{2,1,0:T(8,128)(2,1)}, f32[1,2,512]{2,1,0:T(2,128)}) custom-call(s32[2]{0:T(128)} %offsets_ref.1, s32[1,2]{1,0:T(1,128)} %pairs_ref.1, f32[128]{0:T(128)} %occupied_ref.1, f32[512]{0:T(512)} %energy_ref.1, f32[1,512]{1,0:T(1,128)} %bitcast.1, bf16[64,128,2048]{2,1,0:T(8,128)(2,1)} %factors_ref.3, ...), custom_call_target="tpu_custom_call" | custom-call | tf_op jit(solution)/shard_map/pallas_call | solution.py:51
  4.2 108.0 %shard_map.78 = (f32[1,2,512]{2,1,0:T(2,128)}, f32[1,2,512]{2,1,0:T(2,128)}, bf16[64,128,1024]{2,1,0:T(8,128)(2,1)}) custom-call(bf16[2,128,2048]{2,1,0:T(8,128)(2,1)} %get-tuple-element.7.rows_ref, bf16[1,512,512]{2,1,0:T(8,128)(2,1)} %get-tuple-element.8.turned_ref, f32[1,2,512]{2,1,0:T(2,128)} %get-tuple-element.9.den_ref, bf16[64,128,2048]{2,1,0:T(8,128)(2,1)} %factors_ref.3), custom_call_target="tpu_custom_call" | custom-call | tf_op jit(solution)/shard_map/pallas_call | solution.py:556
  112.2 1.3 %copy.10 = f32[1,2,512]{2,1,0:T(2,128)} copy(f32[1,2,512]{2,1,0:T(2,128)} %get-tuple-element.14) | data formatting | bytes 8192
  113.5 1.3 %copy.11 = f32[1,2,512]{2,1,0:T(2,128)} copy(f32[1,2,512]{2,1,0:T(2,128)} %get-tuple-element.15) | data formatting | bytes 8192

commit v2 on v1

--- a/solution.py
+++ b/solution.py
@@ -66,8 +66,8 @@
 
 def ladder_kernel(
     pair_count, tile_count, sub, width,
-    rows_ref, turned_ref, den_ref, factors_ref,
-    res_ref, upd_ref, land_ref,
+    rows_ref, turned_ref, factors_ref,
+    res_ref, land_ref,
     full, core_buf, own_buf, up_buf, down_buf, up_out, down_out,
     taus, sorted_taus, stage_buf, table, swap, half_made, acc, part, inbox,
     core_sems, up_sems, down_sems, peer_sems,
@@ -109,9 +109,23 @@
         return other // tile_count, lax.rem(other, tile_count)
 
     barrier = pltpu.get_barrier_semaphore()
-    for offset in range(1, total):
-        pl.semaphore_signal(barrier, inc=1, device_id=place(offset), device_id_type=MESH)
-    pl.semaphore_wait(barrier, total - 1)
+    shifts = [shift for shift in (-2, -1, 1, 2) if abs(shift) < stages]
+
+    def in_range(shift):
+        return jnp.logical_and(stage + shift >= 0, stage + shift < stages)
+
+    for device in [mate] + peers:
+        pl.semaphore_signal(barrier, inc=1, device_id=device, device_id_type=MESH)
+    expected = pair_count
+    for shift in shifts:
+        @pl.when(in_range(shift))
+        def _():
+            pl.semaphore_signal(
+                barrier, inc=1, device_id=(p, t + 2 * shift), device_id_type=MESH
+            )
+
+        expected += in_range(shift).astype(jnp.int32)
+    pl.semaphore_wait(barrier, expected)
 
     mine_lanes = pl.ds(pl.multiple_of(core * half, half), half)
     mate_lanes = pl.ds(pl.multiple_of((1 - core) * half, half), half)
@@ -159,11 +173,6 @@
 
     def tau_spot(tile, i):
         return taus.at[pl.ds(tile * block, block), group(i)]
-
-    shifts = [shift for shift in (-2, -1, 1, 2) if abs(shift) < stages]
-
-    def in_range(shift):
-        return jnp.logical_and(stage + shift >= 0, stage + shift < stages)
 
     def direct_copy(d, i):
         return pltpu.make_async_remote_copy(
@@ -258,15 +267,16 @@
             mate_load(n - steps, n % slots).wait()
             sort_slab(n - steps, n % slots, 1 - core)
 
-    first = steps + steps // 2
-    early_slabs = steps - steps // 2 + 1
+    slabs = 2 * steps
+    own_steps = dict(zip((0, 2, 4, 6, 9), range(steps)))
+    relay_steps = dict(zip((3, 5, 7, 10), range(steps)))
 
     for h in range(count):
         core_copy(h).start()
     for j in range(pair_count - 1):
         plane_copy(j).start()
     plane_keep().start()
-    for i in range(min(early_slabs, steps)):
+    for i in range(steps):
         slab_copy(i).start()
     for n in range(slots - 1):
         load_slab(n)
@@ -378,55 +388,46 @@
             forward(step - lag)
         if 0 <= step - 2 * lag < count:
             forward_far(step - 2 * lag)
-        if step == 1:
+        if step == 0:
             for j in range(pair_count - 1):
                 plane_copy(j).wait_recv()
             plane_keep().wait()
-            send_own(0)
-        if step == 4:
-            send_own(1)
-        if step == count - 1:
-            send_own(2)
-            relay(0)
-        if sorted_count < first:
-            if sorted_count + slots - 1 < first:
+        if step in own_steps:
+            send_own(own_steps[step])
+        if step in relay_steps:
+            relay(relay_steps[step])
+        if sorted_count < slabs:
+            if sorted_count + slots - 1 < slabs:
                 load_slab(sorted_count + slots - 1)
             finish_slab(sorted_count)
             sorted_count += 1
-    while sorted_count < first:
-        if sorted_count + slots - 1 < first:
+    while sorted_count < slabs:
+        if sorted_count + slots - 1 < slabs:
             load_slab(sorted_count + slots - 1)
         finish_slab(sorted_count)
         sorted_count += 1
+    collect(0)
 
     blocks = pairs // GROUP
     many = width // both_b
     tile = half_made.shape[-1]
 
     def main(i, carry):
-        @pl.when(i + 3 < steps)
-        def _():
-            send_own(i + 3)
-
-        @pl.when(i + 1 < steps)
-        def _():
-            relay(i + 1)
-
-        collect(i)
-
-        @pl.when(i + early_slabs < steps)
-        def _():
-            slab_copy(i + early_slabs).start()
-
-        late_slab = i + first - steps
-
-        @pl.when(late_slab < steps)
-        def _():
-            slab_copy(late_slab).wait_recv()
-            mate_load(late_slab, 0).start()
+        @pl.when(i + len(own_steps) < steps)
+        def _():
+            send_own(i + len(own_steps))
 
         for source in range(stages):
             mate_copy(source, i).wait_recv()
+
+        @pl.when(jnp.logical_and(i + 2 >= len(relay_steps), i + 2 < steps))
+        def _():
+            relay(i + 2)
+
+        @pl.when(i + 1 < steps)
+        def _():
+            collect(i + 1)
+
         for s in range(blocks):
             rows = taus[s * GROUP : (s + 1) * GROUP, group(i), :].reshape(spread, -1)
             sorted_taus[s] = jnp.dot(swap[...], rows, preferred_element_type=F32).astype(taus.dtype)
@@ -452,11 +453,6 @@
 
         lax.fori_loop(0, half // tile, part_of, 0)
 
-        @pl.when(late_slab < steps)
-        def _():
-            mate_load(late_slab, 0).wait()
-            sort_slab(late_slab, 0, 1 - core)
-
         return carry
 
     lax.fori_loop(0, steps, main, 0)
@@ -527,17 +523,28 @@
                 if tile_index > 2 * z or source:
                     value += inbox[tile_index, source]
         res_ref[:, :, z * both_b : (z + 1) * both_b] = value
-    upd_ref[...] = res_ref[...] / den_ref[...]
-
-
-def ladder(rows, turned, den, factors, pair_count, tile_count):
+
+
+def settle_kernel(sum_ref, den_ref, res_ref, upd_ref):
+    res_ref[...] = sum_ref[...]
+    upd_ref[...] = sum_ref[...] / den_ref[...]
+
+
+def settle(sums, den):
+    shape = jax.ShapeDtypeStruct(sums.shape, F32)
+    return pl.pallas_call(
+        settle_kernel, out_shape=(shape, shape), in_specs=[VMEM, VMEM], out_specs=(VMEM, VMEM)
+    )(sums, den)
+
+
+def ladder(rows, turned, factors, pair_count, tile_count):
     window, cols, aux = rows.shape
     half = aux // 2
     own_b, own_d, _ = factors.shape
     local_pairs, virt, _ = turned.shape
     pairs = pair_count * tile_count * local_pairs
     both_b = 2 * own_b
-    width = max(256, both_b)
+    width = max(512, both_b)
     many = width // both_b
     sub = max(16, cols // 4)
     count = window * cols // sub
@@ -555,9 +562,9 @@
     slots = 3
     return pl.pallas_call(
         functools.partial(ladder_kernel, pair_count, tile_count, sub, width),
-        out_shape=(shape, shape, jax.ShapeDtypeStruct((own_b, own_d, half), kind)),
-        in_specs=[VMEM, VMEM, VMEM, hbm],
-        out_specs=(VMEM, VMEM, pl.BlockSpec(memory_space=pltpu.HBM)),
+        out_shape=(shape, jax.ShapeDtypeStruct((own_b, own_d, half), kind)),
+        in_specs=[VMEM, VMEM, hbm],
+        out_specs=(VMEM, pl.BlockSpec(memory_space=pltpu.HBM)),
         scratch_shapes=[pltpu.VMEM((window, pair_count, cols, half), kind)]
         + [piece] * 6
         + [
@@ -577,7 +584,7 @@
         compiler_params=pltpu.CompilerParams(
             collective_id=0, has_side_effects=True, vmem_limit_bytes=63 * 1024 * 1024
         ),
-    )(rows, turned, den, factors)
+    )(rows, turned, factors)
 
 
 def local(amplitudes, factors, pair_list, window_offsets, occupied_energy, virtual_energy):
@@ -586,8 +593,8 @@
     rows, turned, den = prepare(
         amplitudes, factors, pair_list, window_offsets, occupied_energy, virtual_energy
     )
-    residual, update, _ = ladder(rows, turned, den, factors, pair_count, tile_count)
-    return residual, update
+    sums, _ = ladder(rows, turned, factors, pair_count, tile_count)
+    return settle(sums, den)
 
 
 def solution(mesh):

time: 115 us -> 91.2 us (0.79)
  Pallas kernels: 112 us -> 90.3 us
  local copies, waits for them, and re-layouts: 2.53 us -> 0 us
    pallas_call x1, Pallas kernels: 108 us -> 85.5 us  [ladder(): pl.pallas_call(functools.partial(ladder_kernel, pair_count, tile_count, s...]
    unnamed x2 -> x0, local copies, waits for them, and re-layouts: 2.53 us -> none
    pallas_call x0 -> x1, Pallas kernels: none -> 1.28 us  [settle(): pl.pallas_call(settle_kernel, out_shape=(shape, shape), in_specs=[VMEM, V...]
where the time goes in v2:
time: 91.2 us; the launch traced here: 90.9 us
  Pallas kernels  90.3 us (99%)
    pallas_call x1, Pallas kernels, ladder(): pl.pallas_call(functools.partial(ladder_kernel, pair_count, tile_count, s...  85.5 us
    pallas_call x1, Pallas kernels, prepare(): pl.pallas_call(prepare_kernel, out_shape=(jax.ShapeDtypeStruct((window,)...  3.52 us

profile of v2, /device:TPU:0, one launch (start us, length us, event | category | flops | bytes accessed | tf_op | source)
XLA Modules:
  0.0 90.9 jit_solution(14250528066678416676)
XLA Ops:
  0.6 3.5 %shard_map.77 = (bf16[2,128,2048]{2,1,0:T(8,128)(2,1)}, bf16[1,512,512]{2,1,0:T(8,128)(2,1)}, f32[1,2,512]{2,1,0:T(2,128)}) custom-call(s32[2]{0:T(128)} %offsets_ref.1, s32[1,2]{1,0:T(1,128)} %pairs_ref.1, f32[128]{0:T(128)} %occupied_ref.1, f32[512]{0:T(512)} %energy_ref.1, f32[1,512]{1,0:T(1,128)} %bitcast.1, bf16[64,128,2048]{2,1,0:T(8,128)(2,1)} %factors_ref.3, ...), custom_call_target="tpu_custom_call" | custom-call | tf_op jit(solution)/shard_map/pallas_call | solution.py:51
  4.2 85.5 %shard_map.78 = (f32[1,2,512]{2,1,0:T(2,128)}, bf16[64,128,1024]{2,1,0:T(8,128)(2,1)}) custom-call(bf16[2,128,2048]{2,1,0:T(8,128)(2,1)} %get-tuple-element.6.rows_ref, bf16[1,512,512]{2,1,0:T(8,128)(2,1)} %get-tuple-element.7.turned_ref, bf16[64,128,2048]{2,1,0:T(8,128)(2,1)} %factors_ref.3), custom_call_target="tpu_custom_call" | custom-call | tf_op jit(solution)/shard_map/pallas_call | solution.py:563
  89.7 1.3 %shard_map.79 = (f32[1,2,512]{2,1,0:T(2,128)}, f32[1,2,512]{2,1,0:T(2,128)}) custom-call(f32[1,2,512]{2,1,0:T(2,128)} %get-tuple-element.8.sum_ref, f32[1,2,512]{2,1,0:T(2,128)} %get-tuple-element.9.den_ref), custom_call_target="tpu_custom_call" | custom-call | tf_op jit(solution)/shard_map/pallas_call | solution.py:535

commit v3 on v2

--- a/solution.py
+++ b/solution.py
@@ -10,8 +10,11 @@
 MESH = pl.DeviceIdType.MESH
 VMEM = pl.BlockSpec(memory_space=pltpu.VMEM)
 SMEM = pl.BlockSpec(memory_space=pltpu.SMEM)
+HBM = pl.BlockSpec(memory_space=pltpu.HBM)
 F32 = jnp.float32
 GROUP = 16
+OWN_STEPS = (4, 6, 7, 8, 9, 10, 11)
+RELAY_STEPS = (8, 10, 11)
 
 
 def prepare_kernel(
@@ -55,7 +58,7 @@
             jax.ShapeDtypeStruct(amplitudes.shape, amplitudes.dtype),
             jax.ShapeDtypeStruct((local_pairs, window, virt), F32),
         ),
-        in_specs=[SMEM, SMEM, SMEM, SMEM, VMEM, pl.BlockSpec(memory_space=pl.ANY), VMEM],
+        in_specs=[SMEM, SMEM, SMEM, SMEM, VMEM, HBM, VMEM],
         out_specs=(VMEM, VMEM, VMEM),
         scratch_shapes=[pltpu.SemaphoreType.DMA((window,))],
     )(
@@ -67,12 +70,12 @@
 def ladder_kernel(
     pair_count, tile_count, sub, width,
     rows_ref, turned_ref, factors_ref,
-    res_ref, land_ref,
+    res_ref,
     full, core_buf, own_buf, up_buf, down_buf, up_out, down_out,
-    taus, sorted_taus, stage_buf, table, swap, half_made, acc, part, inbox,
-    core_sems, up_sems, down_sems, peer_sems,
-    plane_sems, direct_sems, arrive_sems, relay_sems, mate_sems,
-    slab_sems, stage_sems, settle_sems, local_sems,
+    taus, sorted_taus, table, swap, half_made, acc, part, inbox,
+    sent_sems, core_sems, up_sems, down_sems, peer_sems,
+    plane_sems, direct_sems, arrive_sems, relay_sems, mate_sent, mate_sems,
+    slab_sent, slab_sems, load_sems, settle_sems, local_sems,
 ):
     p = lax.axis_index("pair")
     t = lax.axis_index("vtile")
@@ -134,41 +137,49 @@
 
     def remote(src, dst, sems, index, device):
         return pltpu.make_async_remote_copy(
-            src_ref=src, dst_ref=dst, send_sem=sems.at[(0,) + index], recv_sem=sems.at[(1,) + index],
+            src_ref=src, dst_ref=dst, send_sem=sems[0], recv_sem=sems[1].at[index],
             device_id=device, device_id_type=MESH,
         )
 
+    def all_sent(ref, sem):
+        pltpu.make_async_remote_copy(
+            src_ref=ref, dst_ref=ref, send_sem=sem, recv_sem=sem,
+            device_id=mate, device_id_type=MESH,
+        ).wait_recv()
+
     def group(i):
         return pl.ds(pl.multiple_of(i * GROUP, GROUP), GROUP)
 
     def core_copy(h):
         k, rows = chunks[h]
-        return remote(rows_ref.at[k, rows, mate_lanes], core_buf.at[k, rows], core_sems, (h,), mate)
+        return remote(rows_ref.at[k, rows, mate_lanes], core_buf.at[k, rows], (sent_sems.at[0], core_sems), (h,), mate)
 
     def up_copy(h):
         k, rows = chunks[h]
-        return remote(up_out.at[k, rows], up_buf.at[k, rows], up_sems, (h,), above)
+        return remote(up_out.at[k, rows], up_buf.at[k, rows], (sent_sems.at[1], up_sems), (h,), above)
 
     def down_copy(h):
         k, rows = chunks[h]
-        return remote(down_out.at[k, rows], down_buf.at[k, rows], down_sems, (h,), below)
+        return remote(down_out.at[k, rows], down_buf.at[k, rows], (sent_sems.at[2], down_sems), (h,), below)
 
     def peer_copy(h, j):
         k, rows = chunks[h]
         if j >= near:
             spot = full.at[k, sources[h % 2], rows]
-            return remote(spot, spot, peer_sems, (j, h), peers[1 - h % 2])
+            return remote(spot, spot, (sent_sems.at[4 + j], peer_sems), (j, h), peers[1 - h % 2])
         spot = full.at[k, p, rows]
-        return remote(spot, spot, peer_sems, (j, h), peers[j])
+        return remote(spot, spot, (sent_sems.at[4 + j], peer_sems), (j, h), peers[j])
 
     def plane_copy(j):
-        rows = pl.ds(pl.multiple_of(peers[j][0] * own_d, own_d), own_d)
-        spot = taus.at[pl.ds((t * pair_count + p) * local_pairs, local_pairs)]
-        return remote(turned_ref.at[:, rows], spot, plane_sems, (j,), peers[j])
+        there = peers[j][0]
+        rows = pl.ds(pl.multiple_of(there * own_d, own_d), own_d)
+        turn = lax.rem(p - there + pair_count, pair_count)
+        spot = taus.at[pl.ds((t * pair_count + turn) * local_pairs, local_pairs)]
+        return remote(turned_ref.at[:, rows], spot, (sent_sems.at[3], plane_sems), (0,), peers[j])
 
     def plane_keep():
         rows = pl.ds(pl.multiple_of(p * own_d, own_d), own_d)
-        spot = taus.at[pl.ds((t * pair_count + p) * local_pairs, local_pairs)]
+        spot = taus.at[pl.ds(t * block, local_pairs)]
         return pltpu.make_async_copy(turned_ref.at[:, rows], spot, local_sems.at[0])
 
     def tau_spot(tile, i):
@@ -177,7 +188,7 @@
     def direct_copy(d, i):
         return pltpu.make_async_remote_copy(
             src_ref=tau_spot(t, i), dst_ref=tau_spot(t, i),
-            send_sem=direct_sems.at[d, i], recv_sem=arrive_sems.at[stage, i],
+            send_sem=direct_sems.at[d], recv_sem=arrive_sems.at[stage, i],
             device_id=(p, t + 2 * shifts[d]), device_id_type=MESH,
         )
 
@@ -185,19 +196,22 @@
         spot = tau_spot(2 * source + core, i)
         return pltpu.make_async_remote_copy(
             src_ref=spot, dst_ref=spot,
-            send_sem=relay_sems.at[source, i], recv_sem=arrive_sems.at[source, i],
+            send_sem=relay_sems.at[source], recv_sem=arrive_sems.at[source, i],
             device_id=(p, t + 2 * shift), device_id_type=MESH,
         )
 
     def mate_copy(source, i):
         spot = tau_spot(2 * source + core, i)
-        return remote(spot, spot, mate_sems, (source, i), mate)
+        return remote(spot, spot, (mate_sent.at[source], mate_sems), (i,), mate)
 
     def goes_up(source):
         return jnp.logical_and(stage >= source + 2, stage + 1 < stages)
 
     def goes_down(source):
         return jnp.logical_and(stage <= source - 2, stage >= 1)
+
+    def mate_wait(i):
+        all_sent(taus.at[pl.ds(0, stages * block), group(i)], mate_sems.at[i])
 
     def send_own(i):
         for d, shift in enumerate(shifts):
@@ -227,49 +241,36 @@
 
             mate_copy(source, i).start()
 
-    def slab_copy(i):
-        return remote(
-            factors_ref.at[:, group(i), mate_lanes], land_ref.at[:, group(i)], slab_sems, (i,), mate
+    def mate_slab(i):
+        return remote(factors_ref.at[:, group(i), mate_lanes], table.at[core, i], (slab_sent.at[i], slab_sems), (i,), mate)
+
+    def own_slab(i):
+        return pltpu.make_async_copy(
+            factors_ref.at[:, group(i), mine_lanes], table.at[core, i], load_sems.at[i]
         )
 
-    slots = stage_buf.shape[0]
-
-    def own_load(i, slot):
-        return pltpu.make_async_copy(
-            factors_ref.at[:, group(i), mine_lanes], stage_buf.at[slot], stage_sems.at[slot]
-        )
-
-    def mate_load(i, slot):
-        return pltpu.make_async_copy(land_ref.at[:, group(i)], stage_buf.at[slot], stage_sems.at[slot])
-
-    def sort_slab(i, slot, side):
+    def sort_slab(side, i):
         def one(b, carry):
-            rows = stage_buf[slot, group(b)].reshape(GROUP * GROUP, half)
+            rows = table[side, i, group(b)].reshape(spread, half)
             made = jnp.dot(swap[...], rows, preferred_element_type=F32).astype(table.dtype)
-            spot = pl.ds(pl.multiple_of(side * own_b + b * GROUP, GROUP), GROUP)
-            table[group(i), spot, :] = made.reshape(GROUP, GROUP, half)
+            table[side, i, group(b)] = made.reshape(GROUP, GROUP, half)
             return carry
 
         lax.fori_loop(0, own_b // GROUP, one, 0)
-
-    def load_slab(n):
-        if n < steps:
-            own_load(n, n % slots).start()
-        else:
-            slab_copy(n - steps).wait_recv()
-            mate_load(n - steps, n % slots).start()
 
     def finish_slab(n):
         if n < steps:
-            own_load(n, n % slots).wait()
-            sort_slab(n, n % slots, core)
+            own_slab(n).wait()
+            sort_slab(core, n)
         else:
-            mate_load(n - steps, n % slots).wait()
-            sort_slab(n - steps, n % slots, 1 - core)
+            mate_slab(n - steps).wait_recv()
+            sort_slab(1 - core, n - steps)
 
     slabs = 2 * steps
-    own_steps = dict(zip((0, 2, 4, 6, 9), range(steps)))
-    relay_steps = dict(zip((3, 5, 7, 10), range(steps)))
+    own_steps = dict(zip(OWN_STEPS, range(steps)))
+    relay_steps = dict(zip(RELAY_STEPS, range(steps)))
+    relays = len(relay_steps)
+    sends = len(own_steps)
 
     for h in range(count):
         core_copy(h).start()
@@ -277,9 +278,8 @@
         plane_copy(j).start()
     plane_keep().start()
     for i in range(steps):
-        slab_copy(i).start()
-    for n in range(slots - 1):
-        load_slab(n)
+        own_slab(i).start()
+        mate_slab(i).start()
     lanes = lax.broadcasted_iota(jnp.int32, (spread, spread), 1)
     lines = lax.broadcasted_iota(jnp.int32, (spread, spread), 0)
     swap[...] = jnp.where(
@@ -389,23 +389,20 @@
         if 0 <= step - 2 * lag < count:
             forward_far(step - 2 * lag)
         if step == 0:
-            for j in range(pair_count - 1):
-                plane_copy(j).wait_recv()
+            all_sent(taus.at[pl.ds(t * block + local_pairs, block - local_pairs)], plane_sems.at[0])
             plane_keep().wait()
         if step in own_steps:
             send_own(own_steps[step])
         if step in relay_steps:
             relay(relay_steps[step])
         if sorted_count < slabs:
-            if sorted_count + slots - 1 < slabs:
-                load_slab(sorted_count + slots - 1)
             finish_slab(sorted_count)
             sorted_count += 1
     while sorted_count < slabs:
-        if sorted_count + slots - 1 < slabs:
-            load_slab(sorted_count + slots - 1)
         finish_slab(sorted_count)
         sorted_count += 1
+    for i in range(relays, min(2, steps)):
+        relay(i)
     collect(0)
 
     blocks = pairs // GROUP
@@ -413,14 +410,13 @@
     tile = half_made.shape[-1]
 
     def main(i, carry):
-        @pl.when(i + len(own_steps) < steps)
-        def _():
-            send_own(i + len(own_steps))
-
-        for source in range(stages):
-            mate_copy(source, i).wait_recv()
-
-        @pl.when(jnp.logical_and(i + 2 >= len(relay_steps), i + 2 < steps))
+        @pl.when(i + sends < steps)
+        def _():
+            send_own(i + sends)
+
+        mate_wait(i)
+
+        @pl.when(jnp.logical_and(i + 2 >= relays, i + 2 < steps))
         def _():
             relay(i + 2)
 
@@ -443,7 +439,13 @@
                     half_made[u, k] = made[:, u]
             added = acc[...]
             for u in range(GROUP // many):
-                right = table[pl.ds(i * GROUP + u * many, many), :, qs].reshape(width, tile)
+                right = jnp.concatenate(
+                    [
+                        table[side, i, b + u * many : b + (u + 1) * many, :, qs].reshape(-1, tile)
+                        for side in range(2)
+                        for b in range(0, own_b, GROUP)
+                    ]
+                )
                 added += lax.dot_general(
                     half_made[u].reshape(-1, tile), right, (((1,), (1,)), ((), ())),
                     preferred_element_type=F32,
@@ -457,65 +459,70 @@
 
     lax.fori_loop(0, steps, main, 0)
 
+    lines = lax.broadcasted_iota(jnp.int32, (width, both_b), 0)
+    lanes = lax.broadcasted_iota(jnp.int32, (width, both_b), 1)
+    same_block = lines // (many * GROUP) == lanes // GROUP
+    choose = jnp.where(jnp.logical_and(same_block, lines % GROUP == lanes % GROUP), 1.0, 0.0)
+    which = lax.broadcasted_iota(jnp.int32, (GROUP, width), 1) // GROUP % many
     for k in range(window):
         for s in range(blocks):
             base = (k * blocks + s) * many * GROUP
-            value = acc[base : base + GROUP, 0:both_b]
+            value = jnp.where(which == 0, acc[base : base + GROUP, :], 0.0)
             for u in range(1, many):
-                value += acc[base + u * GROUP : base + (u + 1) * GROUP, u * both_b : (u + 1) * both_b]
-            part[s * GROUP : (s + 1) * GROUP, k, :] = value
+                rows = acc[base + u * GROUP : base + (u + 1) * GROUP, :]
+                value += jnp.where(which == u, rows, 0.0)
+            part[s * GROUP : (s + 1) * GROUP, k, :] = jnp.dot(
+                value, choose, precision=lax.Precision.HIGHEST, preferred_element_type=F32
+            )
 
     def settle_copy(offset):
         there = place(offset)
-        spot = pl.ds((there[1] * pair_count + there[0]) * local_pairs, local_pairs)
+        turn = lax.rem(there[0] - p + pair_count, pair_count)
+        spot = pl.ds((there[1] * pair_count + turn) * local_pairs, local_pairs)
         return pltpu.make_async_remote_copy(
             src_ref=part.at[spot], dst_ref=inbox.at[t, p],
-            send_sem=settle_sems.at[0, offset], recv_sem=settle_sems.at[1, offset],
+            send_sem=settle_sems.at[0], recv_sem=settle_sems.at[1],
             device_id=there, device_id_type=MESH,
         )
 
     for offset in range(1, total):
         settle_copy(offset).start()
-    spot = pl.ds((t * pair_count + p) * local_pairs, local_pairs)
+    spot = pl.ds(t * block, local_pairs)
     settle_keep = pltpu.make_async_copy(part.at[spot], inbox.at[t, p], local_sems.at[1])
     settle_keep.start()
 
-    for h in range(count):
-        core_copy(h).wait_send()
-
-        @pl.when(stage < stages - 1)
-        def _():
-            up_copy(h).wait_send()
-
-        @pl.when(stage > 0)
-        def _():
-            down_copy(h).wait_send()
-
-        for j in range(pair_count - 1):
-            peer_copy(h, j).wait_send()
+    all_sent(core_buf, sent_sems.at[0])
+
+    @pl.when(stage < stages - 1)
+    def _():
+        all_sent(up_out, sent_sems.at[1])
+
+    @pl.when(stage > 0)
+    def _():
+        all_sent(down_out, sent_sems.at[2])
+
+    all_sent(taus.at[pl.ds(0, block - local_pairs)], sent_sems.at[3])
+    for i in range(steps):
+        mate_slab(i).wait_send()
     for j in range(pair_count - 1):
-        plane_copy(j).wait_send()
-
-    def drain(i, carry):
-        slab_copy(i).wait_send()
-        for d, shift in enumerate(shifts):
-            @pl.when(in_range(shift))
-            def _():
-                direct_copy(d, i).wait_send()
-
-        for source in range(stages):
-            mate_copy(source, i).wait_send()
-
-            @pl.when(jnp.logical_or(goes_up(source), goes_down(source)))
-            def _():
-                relay_copy(source, i, 1).wait_send()
-
-        return carry
-
-    lax.fori_loop(0, steps, drain, 0)
+        all_sent(own_buf, sent_sems.at[4 + j])
+    tile_taus = taus.at[pl.ds(0, block)]
+    for d, shift in enumerate(shifts):
+        @pl.when(in_range(shift))
+        def _():
+            all_sent(tile_taus, direct_sems.at[d])
+
+    for source in range(stages):
+        all_sent(tile_taus, mate_sent.at[source])
+
+        @pl.when(jnp.logical_or(goes_up(source), goes_down(source)))
+        def _():
+            all_sent(tile_taus, relay_sems.at[source])
+
     settle_keep.wait()
-    for offset in range(1, total):
-        settle_copy(offset).wait()
+    others = part.at[pl.ds(0, (total - 1) * local_pairs)]
+    all_sent(others, settle_sems.at[0])
+    all_sent(others, settle_sems.at[1])
     for z in range(stages):
         value = inbox[2 * z, 0]
         for tile_index in (2 * z, 2 * z + 1):
@@ -533,7 +540,7 @@
 def settle(sums, den):
     shape = jax.ShapeDtypeStruct(sums.shape, F32)
     return pl.pallas_call(
-        settle_kernel, out_shape=(shape, shape), in_specs=[VMEM, VMEM], out_specs=(VMEM, VMEM)
+        settle_kernel, out_shape=(shape, shape), in_specs=[VMEM, VMEM], out_specs=(VMEM, VMEM),
     )(sums, den)
 
 
@@ -552,34 +559,32 @@
     stages = tile_count // 2
     spread = GROUP * GROUP
     blocks = pairs // GROUP
-    tile = min(512, half)
+    tile = min(1024, half)
     total = pair_count * tile_count
     kind = rows.dtype
     dma = pltpu.SemaphoreType.DMA
-    hbm = pl.BlockSpec(memory_space=pl.ANY)
     piece = pltpu.VMEM((window, cols, half), kind)
     shape = jax.ShapeDtypeStruct((local_pairs, window, virt), F32)
-    slots = 3
     return pl.pallas_call(
         functools.partial(ladder_kernel, pair_count, tile_count, sub, width),
-        out_shape=(shape, jax.ShapeDtypeStruct((own_b, own_d, half), kind)),
-        in_specs=[VMEM, VMEM, hbm],
-        out_specs=(VMEM, pl.BlockSpec(memory_space=pltpu.HBM)),
+        out_shape=shape,
+        in_specs=[VMEM, VMEM, HBM],
+        out_specs=VMEM,
         scratch_shapes=[pltpu.VMEM((window, pair_count, cols, half), kind)]
         + [piece] * 6
         + [
             pltpu.VMEM((pairs, own_d, virt), kind),
             pltpu.VMEM((blocks, spread, virt), kind),
-            pltpu.VMEM((slots, own_b, GROUP, half), kind),
-            pltpu.VMEM((own_d, both_b, half), kind),
+            pltpu.VMEM((2, steps, own_b, GROUP, half), kind),
             pltpu.VMEM((spread, spread), kind),
             pltpu.VMEM((GROUP // many, window, blocks, many * GROUP, tile), kind),
             pltpu.VMEM((window * blocks * many * GROUP, width), F32),
             pltpu.VMEM((pairs, window, both_b), F32),
             pltpu.VMEM((tile_count, pair_count, local_pairs, window, both_b), F32),
-            dma((2, count)), dma((2, count)), dma((2, count)), dma((2, pair_count - 1, count)),
-            dma((2, pair_count - 1)), dma((4, steps)), dma((stages, steps)), dma((stages, steps)),
-            dma((2, stages, steps)), dma((2, steps)), dma((slots,)), dma((2, total)), dma((2,)),
+            dma((3 + pair_count,)), dma((count,)), dma((count,)), dma((count,)),
+            dma((pair_count - 1, count)),
+            dma((1,)), dma((4,)), dma((stages, steps)), dma((stages,)), dma((stages,)),
+            dma((steps,)), dma((steps,)), dma((steps,)), dma((steps,)), dma((2,)), dma((2,)),
         ],
         compiler_params=pltpu.CompilerParams(
             collective_id=0, has_side_effects=True, vmem_limit_bytes=63 * 1024 * 1024
@@ -593,7 +598,7 @@
     rows, turned, den = prepare(
         amplitudes, factors, pair_list, window_offsets, occupied_energy, virtual_energy
     )
-    sums, _ = ladder(rows, turned, factors, pair_count, tile_count)
+    sums = ladder(rows, turned, factors, pair_count, tile_count)
     return settle(sums, den)
 
 

time: 91.2 us -> 81.9 us (0.90)
  Pallas kernels: 90.3 us -> 81.1 us
    pallas_call x1, Pallas kernels: 85.5 us -> 76.2 us  [ladder(): pl.pallas_call(functools.partial(ladder_kernel, pair_count, tile_count, s...]
where the time goes in v3:
time: 81.9 us; the launch traced here: 81.7 us
  Pallas kernels  81.1 us (99%)
    pallas_call x1, Pallas kernels, ladder(): pl.pallas_call(functools.partial(ladder_kernel, pair_count, tile_count, s...  76.2 us
    pallas_call x1, Pallas kernels, prepare(): pl.pallas_call(prepare_kernel, out_shape=(jax.ShapeDtypeStruct((window,)...  3.53 us

profile of v3, /device:TPU:0, one launch (start us, length us, event | category | flops | bytes accessed | tf_op | source)
XLA Modules:
  0.0 81.7 jit_solution(1915689794779728780)
XLA Ops:
  0.6 3.5 %shard_map.77 = (bf16[2,128,2048]{2,1,0:T(8,128)(2,1)}, bf16[1,512,512]{2,1,0:T(8,128)(2,1)}, f32[1,2,512]{2,1,0:T(2,128)}) custom-call(s32[2]{0:T(128)} %offsets_ref.1, s32[1,2]{1,0:T(1,128)} %pairs_ref.1, f32[128]{0:T(128)} %occupied_ref.1, f32[512]{0:T(512)} %energy_ref.1, f32[1,512]{1,0:T(1,128)} %bitcast.1, bf16[64,128,2048]{2,1,0:T(8,128)(2,1)} %factors_ref.3, ...), custom_call_target="tpu_custom_call" | custom-call | tf_op jit(solution)/shard_map/pallas_call | solution.py:54
  4.2 76.2 %shard_map.78.sum_ref = f32[1,2,512]{2,1,0:T(2,128)} custom-call(bf16[2,128,2048]{2,1,0:T(8,128)(2,1)} %get-tuple-element.5.rows_ref, bf16[1,512,512]{2,1,0:T(8,128)(2,1)} %get-tuple-element.6.turned_ref, bf16[64,128,2048]{2,1,0:T(8,128)(2,1)} %factors_ref.3), custom_call_target="tpu_custom_call" | custom-call | tf_op jit(solution)/shard_map/pallas_call | solution.py:568
  80.4 1.3 %shard_map.79 = (f32[1,2,512]{2,1,0:T(2,128)}, f32[1,2,512]{2,1,0:T(2,128)}) custom-call(f32[1,2,512]{2,1,0:T(2,128)} %shard_map.78.sum_ref, f32[1,2,512]{2,1,0:T(2,128)} %get-tuple-element.7.den_ref), custom_call_target="tpu_custom_call" | custom-call | tf_op jit(solution)/shard_map/pallas_call | solution.py:542

commit v4 on v3

--- a/solution.py
+++ b/solution.py
@@ -420,10 +420,6 @@
         def _():
             relay(i + 2)
 
-        @pl.when(i + 1 < steps)
-        def _():
-            collect(i + 1)
-
         for s in range(blocks):
             rows = taus[s * GROUP : (s + 1) * GROUP, group(i), :].reshape(spread, -1)
             sorted_taus[s] = jnp.dot(swap[...], rows, preferred_element_type=F32).astype(taus.dtype)
@@ -437,6 +433,11 @@
                 made = made.reshape(blocks, GROUP // many, many * GROUP, tile)
                 for u in range(GROUP // many):
                     half_made[u, k] = made[:, u]
+
+            @pl.when(jnp.logical_and(j == 0, i + 1 < steps))
+            def _():
+                collect(i + 1)
+
             added = acc[...]
             for u in range(GROUP // many):
                 right = jnp.concatenate(

time: 81.9 us -> 81.8 us (level)
  no operation moved by 1% of the time
where the time goes in v4:
time: 81.8 us; the launch traced here: 81.6 us
  Pallas kernels  81 us (99%)
    pallas_call x1, Pallas kernels, ladder(): pl.pallas_call(functools.partial(ladder_kernel, pair_count, tile_count, s...  76.1 us
    pallas_call x1, Pallas kernels, prepare(): pl.pallas_call(prepare_kernel, out_shape=(jax.ShapeDtypeStruct((window,)...  3.53 us

profile of v4, /device:TPU:0, one launch (start us, length us, event | category | flops | bytes accessed | tf_op | source)
XLA Modules:
  0.0 81.6 jit_solution(14541017299594272428)
XLA Ops:
  0.6 3.5 %shard_map.77 = (bf16[2,128,2048]{2,1,0:T(8,128)(2,1)}, bf16[1,512,512]{2,1,0:T(8,128)(2,1)}, f32[1,2,512]{2,1,0:T(2,128)}) custom-call(s32[2]{0:T(128)} %offsets_ref.1, s32[1,2]{1,0:T(1,128)} %pairs_ref.1, f32[128]{0:T(128)} %occupied_ref.1, f32[512]{0:T(512)} %energy_ref.1, f32[1,512]{1,0:T(1,128)} %bitcast.1, bf16[64,128,2048]{2,1,0:T(8,128)(2,1)} %factors_ref.3, ...), custom_call_target="tpu_custom_call" | custom-call | tf_op jit(solution)/shard_map/pallas_call | solution.py:54
  4.2 76.1 %shard_map.78.sum_ref = f32[1,2,512]{2,1,0:T(2,128)} custom-call(bf16[2,128,2048]{2,1,0:T(8,128)(2,1)} %get-tuple-element.5.rows_ref, bf16[1,512,512]{2,1,0:T(8,128)(2,1)} %get-tuple-element.6.turned_ref, bf16[64,128,2048]{2,1,0:T(8,128)(2,1)} %factors_ref.3), custom_call_target="tpu_custom_call" | custom-call | tf_op jit(solution)/shard_map/pallas_call | solution.py:569
  80.3 1.3 %shard_map.79 = (f32[1,2,512]{2,1,0:T(2,128)}, f32[1,2,512]{2,1,0:T(2,128)}) custom-call(f32[1,2,512]{2,1,0:T(2,128)} %shard_map.78.sum_ref, f32[1,2,512]{2,1,0:T(2,128)} %get-tuple-element.7.den_ref), custom_call_target="tpu_custom_call" | custom-call | tf_op jit(solution)/shard_map/pallas_call | solution.py:543
